TPU v7x, 128 devices: a whole 4x4x4 slice. The times are simulated.
128 devices in a mesh: row: 8 (over z, core), col: 16 (over y, x).
Axes of the slice: x: 4, y: 4, z: 4, core: 2. Of those that a mesh axis runs over, the one named last changes fastest.
Arguments:
- kernel: float32 [16384, 16384], P('row', 'col'), may hold values from 0 to 3, as said below
Outputs:
- trailing: float32 [16384, 16384], P('row', 'col')
- factor_t: float32 [1024, 16384], P('col', 'row')
Inputs may be any that keep to these rules, and one draw needn't show every extreme that they name: K is symmetric: an RBF kernel over 256 donor features plus each donor's noise variance, of 0.5 or more, on the diagonal.
All inputs are finite; a program needn't handle non-finite values.
Results may differ from a plain program's by a relative error of at most 0.0003.
Values sent between devices are 32-bit elements; how exact they have to be, the bound alone decides.
A program may use at most 128 MiB of HBM per device.

v0:
```python
import jax
import jax.numpy as jnp
from jax import lax
from jax.sharding import PartitionSpec as P

PANEL = 512
PANELS = 2


def from_root(value, axis, source):
    kept = jnp.where(lax.axis_index(axis) == source, value, 0).astype(value.dtype)
    return lax.psum(kept, axis)


def outer_update(left_fac, right_fac):
    return lax.dot_general(
        left_fac,
        right_fac,
        (((0,), (0,)), ((), ())),
        precision=lax.Precision.HIGHEST,
        preferred_element_type=jnp.float32,
    )


def local(kernel):
    grid_rows = lax.axis_size("row")
    grid_cols = lax.axis_size("col")
    my_row = lax.axis_index("row")
    my_col = lax.axis_index("col")
    rows_loc = kernel.shape[0]
    cols_loc = kernel.shape[1]
    tile_w = PANEL // grid_cols
    spread = grid_cols // grid_rows
    row_local = jnp.arange(rows_loc, dtype=jnp.int32)
    row_ids = (row_local // tile_w * grid_rows + my_row) * tile_w + row_local % tile_w
    col_local = jnp.arange(cols_loc, dtype=jnp.int32)
    col_ids = (col_local // tile_w * grid_cols + my_col) * tile_w + col_local % tile_w
    down_list = []
    schur = kernel
    for panel_idx in range(PANELS):
        column_tile = schur[:, panel_idx * tile_w : (panel_idx + 1) * tile_w]
        first_col = panel_idx * PANEL
        first_tile = panel_idx * spread
        corner = column_tile[first_tile * tile_w : (first_tile + spread) * tile_w]
        flat_block = corner.reshape(1, spread * tile_w * tile_w)
        blocks = lax.all_gather(flat_block, ("row", "col"), axis=0, tiled=True)
        blocks = blocks.reshape(grid_rows, grid_cols, spread, tile_w, tile_w)
        blocks = blocks.transpose(2, 0, 3, 1, 4).reshape(PANEL, PANEL)
        lower_fac = jnp.linalg.cholesky(blocks)
        columns_t = column_tile.T
        gathered = lax.all_gather(columns_t, "col", axis=0, tiled=True)
        factor_loc = jax.scipy.linalg.solve_triangular(lower_fac, gathered, lower=True)
        factor_loc = jnp.where(row_ids[None, :] >= first_col, factor_loc, 0.0)
        picked = factor_loc.reshape(PANEL, cols_loc // tile_w, spread, tile_w)
        picked = lax.dynamic_index_in_dim(picked, my_col // grid_rows, 2, keepdims=False)
        picked = picked.reshape(PANEL, cols_loc)
        across = from_root(picked, "row", my_col % grid_rows)
        factor_loc, across = (factor_loc, across)
        schur = schur - outer_update(factor_loc, across)
        down_list.append(factor_loc)
    limit = PANELS * PANEL
    keep = (row_ids[:, None] >= limit) & (col_ids[None, :] >= limit)
    trailing = jnp.where(keep, schur, 0.0)
    stacked = jnp.concatenate(down_list, axis=0)
    per_col = PANELS * PANEL // grid_cols
    factor_out = lax.dynamic_slice_in_dim(stacked, my_col * per_col, per_col, 0)
    return (trailing, factor_out)


def solution(mesh):
    return jax.shard_map(
        local,
        mesh=mesh,
        in_specs=(P("row", "col"),),
        out_specs=(P("row", "col"), P("col", "row")),
        check_vma=False,
    )
```

profile of v0, /device:TPU:0, one launch (start us, length us, event | category | flops | bytes accessed | tf_op | source)
XLA Modules:
  0.0 662.9 jit_solution(6436545868017596230)
XLA Ops:
  8.7 9.1 %copy.22 = f32[2048,1024]{0,1:T(8,128)} copy(f32[2048,1024]{1,0:T(8,128)} %param.4) | data formatting | bytes 16777216 | tf_op args[0]
  19.7 57.2 %all-gather.11.cloned.1.call-done = f32[128,1,2048]{2,1,0:T(1,128)} async-done(((f32[1,1,2048]{2,1,0:T(1,128)}), f32[128,1,2048]{2,1,0:T(1,128)}) %all-gather.11.cloned.1.call-update) | async-done | bytes 1048592 | tf_op jit(solution)/shard_map/all_gather | solution.py:46
  76.8 3.7 reduce.16
  83.3 5.6 copy.18
  93.2 11.7 %cholesky.286 = f32[128,128]{1,0:T(8,128)S(1)} custom-call(f32[128,128]{1,0:T(8,128)S(1)} %cholesky.426), custom_call_target="Cholesky" | custom-call | tf_op jit(solution)/shard_map/jit(cholesky)/cholesky | solution.py:49
  105.0 9.8 %custom-call.27 = f32[1,128,128]{1,2,0:T(8,128)S(1)} custom-call(f32[1,128,128]{2,1,0:T(8,128)S(1)} %get-tuple-element.65), custom_call_target="InvertDiagBlocksLowerTriangular" | custom-call | tf_op jit(solution)/shard_map/jit(cholesky)/cholesky | solution.py:49
  115.6 11.7 %cholesky.305 = f32[128,128]{1,0:T(8,128)S(1)} custom-call(f32[128,128]{1,0:T(8,128)S(1)} %cholesky.430), custom_call_target="Cholesky" | custom-call | tf_op jit(solution)/shard_map/jit(cholesky)/cholesky | solution.py:49
  127.3 10.0 %custom-call.28 = f32[1,128,128]{1,2,0:T(8,128)S(1)} custom-call(f32[1,128,128]{2,1,0:T(8,128)S(1)} %get-tuple-element.62), custom_call_target="InvertDiagBlocksLowerTriangular" | custom-call | tf_op jit(solution)/shard_map/jit(cholesky)/cholesky | solution.py:49
  138.0 11.7 %cholesky.326 = f32[128,128]{1,0:T(8,128)S(1)} custom-call(f32[128,128]{1,0:T(8,128)S(1)} %cholesky.435), custom_call_target="Cholesky" | custom-call | tf_op jit(solution)/shard_map/jit(cholesky)/cholesky | solution.py:49
  149.7 9.8 %custom-call.29 = f32[1,128,128]{1,2,0:T(8,128)S(1)} custom-call(f32[1,128,128]{2,1,0:T(8,128)S(1)} %get-tuple-element.59), custom_call_target="InvertDiagBlocksLowerTriangular" | custom-call | tf_op jit(solution)/shard_map/jit(cholesky)/cholesky | solution.py:49
  160.2 11.7 %cholesky.343 = f32[128,128]{1,0:T(8,128)S(1)} custom-call(f32[128,128]{1,0:T(8,128)S(1)} %convolution_subtract_fusion.10), custom_call_target="Cholesky" | custom-call | tf_op jit(solution)/shard_map/jit(cholesky)/cholesky | solution.py:49
  176.5 8.2 %while.4 = (s32[]{:T(128)}, f32[512,512]{1,0:T(8,128)S(1)}, s32[4,2]{0,1:T(2,128)S(1)}, f32[4,128,128]{2,1,0:T(8,128)S(1)}, s32[]{:T(128)}) while((s32[]{:T(128)}, f32[512,512]{1,0:T(8,128)S(1)}, s32[4,2]{0,1:T(2,128)S(1)}, f32[4,128,128]{2,1,0:T(8,128)S(1)}, s32[]{:T(128)}) %tuple.58), condition=%wide.while_cond, body=%wide.while_body.sunk | while | flops 2 | bytes 131181 | solution.py:52
  184.8 39.3 %custom-call.30 = f32[4,128,128]{1,2,0:T(8,128)S(1)} custom-call(f32[4,128,128]{2,1,0:T(8,128)S(1)} %get-tuple-element.18), custom_call_target="InvertDiagBlocksLowerTriangular" | custom-call | tf_op jit(solution)/shard_map/jit(_solve_triangular)/triangular_solve | solution.py:52
  237.8 5.3 copy.21
  246.5 63.6 %all-reduce.4.cloned.1.call-done = f32[512,1024]{0,1:T(8,128)} async-done(((f32[512,1024]{0,1:T(8,128)}), f32[512,1024]{0,1:T(8,128)}) %all-reduce.4.cloned.1.call-update) | async-done | bytes 2097168 | tf_op jit(solution)/shard_map/psum | solution.py:12
  310.2 17.0 %convolution_subtract_fusion = f32[2048,1024]{0,1:T(8,128)S(1)} fusion(f32[2048,1024]{0,1:T(8,128)} %copy.22, f32[512,2048]{1,0:T(8,128)} %maximum_select_fusion, f32[512,1024]{0,1:T(8,128)} %all-reduce.4.cloned.1.call-done), kind=kOutput, calls=%fused_computation.9 | convolution fusion | flops 12886999040 | bytes 23068672 | tf_op jit(solution)/shard_map/dot_general | solution.py:16
  333.3 61.3 %all-gather.13.cloned.1.call-done = f32[128,1,2048]{2,1,0:T(1,128)} async-done(((f32[1,1,2048]{2,1,0:T(1,128)}), f32[128,1,2048]{2,1,0:T(1,128)}) %all-gather.13.cloned.1.call-update) | async-done | bytes 1048592 | tf_op jit(solution)/shard_map/all_gather | solution.py:46
  401.0 5.6 copy.24
  406.6 3.8 reshape.157
  411.0 11.7 %cholesky.358 = f32[128,128]{1,0:T(8,128)S(1)} custom-call(f32[128,128]{1,0:T(8,128)S(1)} %cholesky.439), custom_call_target="Cholesky" | custom-call | tf_op jit(solution)/shard_map/jit(cholesky)/cholesky | solution.py:49
  422.8 9.8 %custom-call.31 = f32[1,128,128]{1,2,0:T(8,128)S(1)} custom-call(f32[1,128,128]{2,1,0:T(8,128)S(1)} %get-tuple-element.55), custom_call_target="InvertDiagBlocksLowerTriangular" | custom-call | tf_op jit(solution)/shard_map/jit(cholesky)/cholesky | solution.py:49
  433.3 11.7 %cholesky.377 = f32[128,128]{1,0:T(8,128)S(1)} custom-call(f32[128,128]{1,0:T(8,128)S(1)} %cholesky.443), custom_call_target="Cholesky" | custom-call | tf_op jit(solution)/shard_map/jit(cholesky)/cholesky | solution.py:49
  445.1 10.2 %custom-call.32 = f32[1,128,128]{1,2,0:T(8,128)S(1)} custom-call(f32[1,128,128]{2,1,0:T(8,128)S(1)} %get-tuple-element.52), custom_call_target="InvertDiagBlocksLowerTriangular" | custom-call | tf_op jit(solution)/shard_map/jit(cholesky)/cholesky | solution.py:49
  455.9 11.7 %cholesky.398 = f32[128,128]{1,0:T(8,128)S(1)} custom-call(f32[128,128]{1,0:T(8,128)S(1)} %cholesky.448), custom_call_target="Cholesky" | custom-call | tf_op jit(solution)/shard_map/jit(cholesky)/cholesky | solution.py:49
  467.7 9.8 %custom-call.33 = f32[1,128,128]{1,2,0:T(8,128)S(1)} custom-call(f32[1,128,128]{2,1,0:T(8,128)S(1)} %get-tuple-element.49), custom_call_target="InvertDiagBlocksLowerTriangular" | custom-call | tf_op jit(solution)/shard_map/jit(cholesky)/cholesky | solution.py:49
  478.1 11.7 %cholesky.415 = f32[128,128]{1,0:T(8,128)S(1)} custom-call(f32[128,128]{1,0:T(8,128)S(1)} %convolution_subtract_fusion.9), custom_call_target="Cholesky" | custom-call | tf_op jit(solution)/shard_map/jit(cholesky)/cholesky | solution.py:49
  495.0 7.6 %while.5 = (s32[]{:T(128)}, f32[512,512]{1,0:T(8,128)S(1)}, s32[4,2]{0,1:T(2,128)S(1)}, f32[4,128,128]{2,1,0:T(8,128)S(1)}, s32[]{:T(128)}) while((s32[]{:T(128)}, f32[512,512]{1,0:T(8,128)S(1)}, s32[4,2]{0,1:T(2,128)S(1)}, f32[4,128,128]{2,1,0:T(8,128)S(1)}, s32[]{:T(128)}) %tuple.76), condition=%wide.while_cond.clone, body=%wide.while_body.clone.sunk | while | flops 2 | bytes 131181 | solution.py:52
  502.7 39.3 %custom-call.34 = f32[4,128,128]{1,2,0:T(8,128)S(1)} custom-call(f32[4,128,128]{2,1,0:T(8,128)S(1)} %get-tuple-element.19), custom_call_target="InvertDiagBlocksLowerTriangular" | custom-call | tf_op jit(solution)/shard_map/jit(_solve_triangular)/triangular_solve | solution.py:52
  555.7 5.3 copy.26
  566.3 61.8 %all-reduce.6.cloned.1.call-done = f32[512,1024]{0,1:T(8,128)} async-done(((f32[512,1024]{0,1:T(8,128)}), f32[512,1024]{0,1:T(8,128)}) %all-reduce.6.cloned.1.call-update) | async-done | bytes 2097168 | tf_op jit(solution)/shard_map/psum | solution.py:12
  628.2 18.4 %subtract_select_fusion = f32[2048,1024]{0,1:T(8,128)} fusion(f32[2048,1024]{0,1:T(8,128)} %copy-done, pred[2048]{0:T(1024)(128)(4,1)S(1)} %broadcast_compare_fusion.1, pred[1024]{0:T(1024)(128)(4,1)S(1)} %fusion.86, f32[512,2048]{1,0:T(8,128)} %maximum_select_fusion.1, f32[512,1024]{0,1:T(8,128)} %all-reduce.6.cloned.1.call-done), kind=kOutput, calls=%fused_computation.6 | convolution fusion | flops 12891193344 | bytes 23071744 | tf_op jit(solution)/shard_map/dot_general | solution.py:16
  646.5 9.2 %copy.28 = f32[2048,1024]{1,0:T(8,128)} copy(f32[2048,1024]{0,1:T(8,128)} %subtract_select_fusion) | data formatting | bytes 16777216
  (123 shorter events, 83.7 us)
Async XLA Ops:
  7.2 69.7 %all-gather.11.cloned.1.call-start = ((), (), s32[]{:S(2)}) async-start(), calls=%async_computation.4 | async-start | bytes 1056768 | tf_op jit(solution)/shard_map/all_gather | solution.py:46
  8.7 215.4 %all-gather.7.cloned.1.call-start = ((), (), s32[]{:S(2)}) async-start(), calls=%async_computation | async-start | bytes 4456448 | tf_op jit(solution)/shard_map/all_gather | solution.py:51
  19.6 290.6 %all-reduce.4.cloned.1.call-start = ((), (), s32[]{:S(2)}) async-start(), calls=%async_computation.1 | async-start | bytes 4194304 | tf_op jit(solution)/shard_map/psum | solution.py:12
  224.1 5.7 copy-start.1
  246.5 148.0 %all-gather.13.cloned.1.call-start = ((), (), s32[]{:S(2)}) async-start(), calls=%async_computation.5 | async-start | bytes 1056768 | tf_op jit(solution)/shard_map/all_gather | solution.py:46
  327.2 3.4 copy-start
  331.5 210.6 %all-gather.9.cloned.1.call-start = ((), (), s32[]{:S(2)}) async-start(), calls=%async_computation.2 | async-start | bytes 4456448 | tf_op jit(solution)/shard_map/all_gather | solution.py:51
  333.2 295.0 %all-reduce.6.cloned.1.call-start = ((), (), s32[]{:S(2)}) async-start(), calls=%async_computation.3 | async-start | bytes 4194304 | tf_op jit(solution)/shard_map/psum | solution.py:12
  542.0 5.7 copy-start.2
Sparse Core Ops, SparseCore 0:
  10.8 65.9 all-gather.10
  79.5 49.2 all-gather.6
  246.6 63.5 all-reduce.3
  331.6 62.9 all-gather.12
  397.1 49.4 all-gather.8
  564.5 63.6 all-reduce.5
where the time goes:
time: 668 us; the launch traced here: 663 us
  other arithmetic  258 us (39%)
  waiting for transfers between devices  244 us (37%)
  local copies, waits for them, and re-layouts  78.7 us (12%)
  matrix products  61.3 us (9%)
  between operations  19.7 us (3%)
    another operation x29, other arithmetic, local(): lower_fac = jnp.linalg.cholesky(blocks)  158 us
    psum x2, waiting for transfers between devices, from_root(): return lax.psum(kept, axis)  125 us
    all_gather x2, waiting for transfers between devices, local(): blocks = lax.all_gather(flat_block, ('row', 'col'), axis=0, tiled=True)  118 us
    another operation x5, other arithmetic, local(): jax.scipy.linalg.solve_triangular(lower_fac, gathered, lower=True)  78.9 us
    dot_general x2, matrix products, outer_update(): lax.dot_general(left_fac, right_fac, (((0,), (0,)), ((), ())), precision=...  35.4 us
    unnamed x10, local copies, waits for them, and re-layouts  23.1 us
    another operation x14, matrix products, local(): jax.scipy.linalg.solve_triangular(lower_fac, gathered, lower=True)  22.2 us
    another operation x27, local copies, waits for them, and re-layouts, local(): jax.scipy.linalg.solve_triangular(lower_fac, gathered, lower=True)  15.5 us
  transfers between devices with their start and end apart: 6, of which 4 were waited for; matrix products, arithmetic and copies ran while one was open for 46% of the time, Pallas kernels for 0%

commit v1 on v0

--- a/solution.py
+++ b/solution.py
@@ -7,9 +7,15 @@
 PANELS = 2
 
 
+def gather_and_add(value, name):
+    parts = lax.all_gather(value, name, axis=0, tiled=False)
+    acc = parts.sum(axis=0)
+    return acc
+
+
 def from_root(value, axis, source):
     kept = jnp.where(lax.axis_index(axis) == source, value, 0).astype(value.dtype)
-    return lax.psum(kept, axis)
+    return gather_and_add(kept, axis)
 
 
 def outer_update(left_fac, right_fac):

time: 668 us -> 727 us (1.088)
  waiting for transfers between devices: 244 us -> 283 us
  other arithmetic: 258 us -> 272 us
    all_gather x0 -> x2, waiting for transfers between devices: none -> 164 us  [gather_and_add(): parts = lax.all_gather(value, name, axis=0, tiled=False)]
    psum x2 -> x0, waiting for transfers between devices: 125 us -> none  [from_root(): return lax.psum(kept, axis)]
    unnamed x0 -> x2, other arithmetic: none -> 15.9 us
  transfers between devices with their start and end apart: 6 -> 6, of which waited for: 4 -> 4; matrix products, arithmetic and copies ran while one was open for 46% -> 42% of each run, Pallas kernels for 0% -> 0%
where the time goes in v1:
time: 727 us; the launch traced here: 720 us
  waiting for transfers between devices  283 us (39%)
  other arithmetic  272 us (37%)
  local copies, waits for them, and re-layouts  83.6 us (11%)
  matrix products  60.6 us (8%)
  between operations  20.3 us (3%)
    all_gather x2, waiting for transfers between devices, gather_and_add(): parts = lax.all_gather(value, name, axis=0, tiled=False)  164 us
    another operation x29, other arithmetic, local(): lower_fac = jnp.linalg.cholesky(blocks)  158 us
    all_gather x2, waiting for transfers between devices, local(): blocks = lax.all_gather(flat_block, ('row', 'col'), axis=0, tiled=True)  119 us
    another operation x5, other arithmetic, local(): jax.scipy.linalg.solve_triangular(lower_fac, gathered, lower=True)  78.9 us
    dot_general x2, matrix products, outer_update(): lax.dot_general(left_fac, right_fac, (((0,), (0,)), ((), ())), precision=...  34.6 us
    unnamed x10, local copies, waits for them, and re-layouts  23.1 us
    another operation x14, matrix products, local(): jax.scipy.linalg.solve_triangular(lower_fac, gathered, lower=True)  22.2 us
    another operation x27, local copies, waits for them, and re-layouts, local(): jax.scipy.linalg.solve_triangular(lower_fac, gathered, lower=True)  16.2 us
  transfers between devices with their start and end apart: 6, of which 4 were waited for; matrix products, arithmetic and copies ran while one was open for 42% of the time, Pallas kernels for 0%

profile of v1, /device:TPU:0, one launch (start us, length us, event | category | flops | bytes accessed | tf_op | source)
XLA Modules:
  0.0 720.1 jit_solution(1605004012382470696)
XLA Ops:
  8.7 9.1 %copy.24 = f32[2048,1024]{0,1:T(8,128)} copy(f32[2048,1024]{1,0:T(8,128)} %param.4) | data formatting | bytes 16777216 | tf_op args[0]
  19.7 57.2 %all-gather.17.cloned.1.call-done = f32[128,1,2048]{2,1,0:T(1,128)} async-done(((f32[1,1,2048]{2,1,0:T(1,128)}), f32[128,1,2048]{2,1,0:T(1,128)}) %all-gather.17.cloned.1.call-update) | async-done | bytes 1048592 | tf_op jit(solution)/shard_map/all_gather | solution.py:52
  83.3 5.6 copy.18
  93.3 11.7 %cholesky.286 = f32[128,128]{1,0:T(8,128)S(1)} custom-call(f32[128,128]{1,0:T(8,128)S(1)} %cholesky.426), custom_call_target="Cholesky" | custom-call | tf_op jit(solution)/shard_map/jit(cholesky)/cholesky | solution.py:55
  105.0 9.8 %custom-call.27 = f32[1,128,128]{1,2,0:T(8,128)S(1)} custom-call(f32[1,128,128]{2,1,0:T(8,128)S(1)} %get-tuple-element.65), custom_call_target="InvertDiagBlocksLowerTriangular" | custom-call | tf_op jit(solution)/shard_map/jit(cholesky)/cholesky | solution.py:55
  115.6 11.7 %cholesky.305 = f32[128,128]{1,0:T(8,128)S(1)} custom-call(f32[128,128]{1,0:T(8,128)S(1)} %cholesky.430), custom_call_target="Cholesky" | custom-call | tf_op jit(solution)/shard_map/jit(cholesky)/cholesky | solution.py:55
  127.4 10.2 %custom-call.28 = f32[1,128,128]{1,2,0:T(8,128)S(1)} custom-call(f32[1,128,128]{2,1,0:T(8,128)S(1)} %get-tuple-element.62), custom_call_target="InvertDiagBlocksLowerTriangular" | custom-call | tf_op jit(solution)/shard_map/jit(cholesky)/cholesky | solution.py:55
  138.2 11.7 %cholesky.326 = f32[128,128]{1,0:T(8,128)S(1)} custom-call(f32[128,128]{1,0:T(8,128)S(1)} %cholesky.435), custom_call_target="Cholesky" | custom-call | tf_op jit(solution)/shard_map/jit(cholesky)/cholesky | solution.py:55
  150.0 9.8 %custom-call.29 = f32[1,128,128]{1,2,0:T(8,128)S(1)} custom-call(f32[1,128,128]{2,1,0:T(8,128)S(1)} %get-tuple-element.59), custom_call_target="InvertDiagBlocksLowerTriangular" | custom-call | tf_op jit(solution)/shard_map/jit(cholesky)/cholesky | solution.py:55
  160.4 11.7 %cholesky.343 = f32[128,128]{1,0:T(8,128)S(1)} custom-call(f32[128,128]{1,0:T(8,128)S(1)} %convolution_subtract_fusion.10), custom_call_target="Cholesky" | custom-call | tf_op jit(solution)/shard_map/jit(cholesky)/cholesky | solution.py:55
  176.8 8.0 %while.4 = (s32[]{:T(128)}, f32[512,512]{1,0:T(8,128)S(1)}, s32[4,2]{0,1:T(2,128)S(1)}, f32[4,128,128]{2,1,0:T(8,128)S(1)}, s32[]{:T(128)}) while((s32[]{:T(128)}, f32[512,512]{1,0:T(8,128)S(1)}, s32[4,2]{0,1:T(2,128)S(1)}, f32[4,128,128]{2,1,0:T(8,128)S(1)}, s32[]{:T(128)}) %tuple.58), condition=%wide.while_cond, body=%wide.while_body.sunk | while | flops 2 | bytes 131181 | solution.py:58
  184.8 39.3 %custom-call.30 = f32[4,128,128]{1,2,0:T(8,128)S(1)} custom-call(f32[4,128,128]{2,1,0:T(8,128)S(1)} %get-tuple-element.18), custom_call_target="InvertDiagBlocksLowerTriangular" | custom-call | tf_op jit(solution)/shard_map/jit(_solve_triangular)/triangular_solve | solution.py:58
  237.8 5.3 copy.21
  247.2 82.6 %all-gather.11.cloned.1.call-done = f32[8,512,1024]{2,1,0:T(8,128)} async-done(((f32[1,512,1024]{2,1,0:T(8,128)}), f32[8,512,1024]{2,1,0:T(8,128)}) %all-gather.11.cloned.1.call-update) | async-done | bytes 16777232 | tf_op jit(solution)/shard_map/all_gather | solution.py:11
  329.8 8.0 %reduce_sum.18 = f32[512,1024]{1,0:T(8,128)S(1)} reduce(f32[8,512,1024]{2,1,0:T(8,128)} %all-gather.11.cloned.1.call-done, f32[]{:T(128)} %constant.217.clone.1), dimensions={0}, to_apply=%region_8.11 | reduce | flops 3670016 | bytes 18874372
  337.8 16.0 %convolution_subtract_fusion = f32[2048,1024]{0,1:T(8,128)S(1)} fusion(f32[2048,1024]{0,1:T(8,128)} %copy.24, f32[512,2048]{1,0:T(8,128)} %maximum_select_fusion, f32[512,1024]{1,0:T(8,128)S(1)} %reduce_sum.18), kind=kOutput, calls=%fused_computation.9 | convolution fusion | flops 12886999040 | bytes 23068672 | tf_op jit(solution)/shard_map/dot_general | solution.py:22
  359.9 62.3 %all-gather.19.cloned.1.call-done = f32[128,1,2048]{2,1,0:T(1,128)} async-done(((f32[1,1,2048]{2,1,0:T(1,128)}), f32[128,1,2048]{2,1,0:T(1,128)}) %all-gather.19.cloned.1.call-update) | async-done | bytes 1048592 | tf_op jit(solution)/shard_map/all_gather | solution.py:52
  428.7 5.6 copy.26
  438.8 11.7 %cholesky.358 = f32[128,128]{1,0:T(8,128)S(1)} custom-call(f32[128,128]{1,0:T(8,128)S(1)} %cholesky.439), custom_call_target="Cholesky" | custom-call | tf_op jit(solution)/shard_map/jit(cholesky)/cholesky | solution.py:55
  450.7 9.8 %custom-call.31 = f32[1,128,128]{1,2,0:T(8,128)S(1)} custom-call(f32[1,128,128]{2,1,0:T(8,128)S(1)} %get-tuple-element.55), custom_call_target="InvertDiagBlocksLowerTriangular" | custom-call | tf_op jit(solution)/shard_map/jit(cholesky)/cholesky | solution.py:55
  461.2 11.7 %cholesky.377 = f32[128,128]{1,0:T(8,128)S(1)} custom-call(f32[128,128]{1,0:T(8,128)S(1)} %cholesky.443), custom_call_target="Cholesky" | custom-call | tf_op jit(solution)/shard_map/jit(cholesky)/cholesky | solution.py:55
  472.9 10.0 %custom-call.32 = f32[1,128,128]{1,2,0:T(8,128)S(1)} custom-call(f32[1,128,128]{2,1,0:T(8,128)S(1)} %get-tuple-element.52), custom_call_target="InvertDiagBlocksLowerTriangular" | custom-call | tf_op jit(solution)/shard_map/jit(cholesky)/cholesky | solution.py:55
  483.6 11.7 %cholesky.398 = f32[128,128]{1,0:T(8,128)S(1)} custom-call(f32[128,128]{1,0:T(8,128)S(1)} %cholesky.448), custom_call_target="Cholesky" | custom-call | tf_op jit(solution)/shard_map/jit(cholesky)/cholesky | solution.py:55
  495.3 9.8 %custom-call.33 = f32[1,128,128]{1,2,0:T(8,128)S(1)} custom-call(f32[1,128,128]{2,1,0:T(8,128)S(1)} %get-tuple-element.49), custom_call_target="InvertDiagBlocksLowerTriangular" | custom-call | tf_op jit(solution)/shard_map/jit(cholesky)/cholesky | solution.py:55
  505.8 11.7 %cholesky.415 = f32[128,128]{1,0:T(8,128)S(1)} custom-call(f32[128,128]{1,0:T(8,128)S(1)} %convolution_subtract_fusion.9), custom_call_target="Cholesky" | custom-call | tf_op jit(solution)/shard_map/jit(cholesky)/cholesky | solution.py:55
  523.3 8.3 %while.5 = (s32[]{:T(128)}, f32[512,512]{1,0:T(8,128)S(1)}, s32[4,2]{0,1:T(2,128)S(1)}, f32[4,128,128]{2,1,0:T(8,128)S(1)}, s32[]{:T(128)}) while((s32[]{:T(128)}, f32[512,512]{1,0:T(8,128)S(1)}, s32[4,2]{0,1:T(2,128)S(1)}, f32[4,128,128]{2,1,0:T(8,128)S(1)}, s32[]{:T(128)}) %tuple.76), condition=%wide.while_cond.clone, body=%wide.while_body.clone.sunk | while | flops 2 | bytes 131181 | solution.py:58
  531.6 39.3 %custom-call.34 = f32[4,128,128]{1,2,0:T(8,128)S(1)} custom-call(f32[4,128,128]{2,1,0:T(8,128)S(1)} %get-tuple-element.19), custom_call_target="InvertDiagBlocksLowerTriangular" | custom-call | tf_op jit(solution)/shard_map/jit(_solve_triangular)/triangular_solve | solution.py:58
  584.7 5.3 copy.28
  596.0 81.0 %all-gather.15.cloned.1.call-done = f32[8,512,1024]{2,1,0:T(8,128)} async-done(((f32[1,512,1024]{2,1,0:T(8,128)}), f32[8,512,1024]{2,1,0:T(8,128)}) %all-gather.15.cloned.1.call-update) | async-done | bytes 16777232 | tf_op jit(solution)/shard_map/all_gather | solution.py:11
  677.0 8.0 %reduce_sum.19 = f32[512,1024]{1,0:T(8,128)S(1)} reduce(f32[8,512,1024]{2,1,0:T(8,128)} %all-gather.15.cloned.1.call-done, f32[]{:T(128)} %constant.217.clone.1), dimensions={0}, to_apply=%region_9.12 | reduce | flops 3670016 | bytes 18874372
  685.0 18.6 %subtract_select_fusion = f32[2048,1024]{0,1:T(8,128)} fusion(f32[2048,1024]{0,1:T(8,128)} %copy-done, pred[2048]{0:T(1024)(128)(4,1)S(1)} %broadcast_compare_fusion.1, pred[1024]{0:T(1024)(128)(4,1)S(1)} %fusion.86, f32[512,2048]{1,0:T(8,128)} %maximum_select_fusion.1, f32[512,1024]{1,0:T(8,128)S(1)} %reduce_sum.19), kind=kOutput, calls=%fused_computation.6 | convolution fusion | flops 12891193344 | bytes 23071744 | tf_op jit(solution)/shard_map/dot_general | solution.py:22
  703.6 9.2 %copy.32 = f32[2048,1024]{1,0:T(8,128)} copy(f32[2048,1024]{0,1:T(8,128)} %subtract_select_fusion) | data formatting | bytes 16777216
  (127 shorter events, 93.8 us)
Async XLA Ops:
  7.2 69.7 %all-gather.17.cloned.1.call-start = ((), (), s32[]{:S(2)}) async-start(), calls=%async_computation.4 | async-start | bytes 1056768 | tf_op jit(solution)/shard_map/all_gather | solution.py:52
  8.7 215.4 %all-gather.9.cloned.1.call-start = ((), (), s32[]{:S(2)}) async-start(), calls=%async_computation | async-start | bytes 4456448 | tf_op jit(solution)/shard_map/all_gather | solution.py:57
  19.6 310.3 %all-gather.11.cloned.1.call-start = ((), (), s32[]{:S(2)}) async-start(), calls=%async_computation.1 | async-start | bytes 18874368 | tf_op jit(solution)/shard_map/all_gather | solution.py:11
  224.1 5.7 copy-start.1
  246.9 175.3 %all-gather.19.cloned.1.call-start = ((), (), s32[]{:S(2)}) async-start(), calls=%async_computation.5 | async-start | bytes 1056768 | tf_op jit(solution)/shard_map/all_gather | solution.py:52
  353.8 3.4 copy-start
  358.1 212.9 %all-gather.13.cloned.1.call-start = ((), (), s32[]{:S(2)}) async-start(), calls=%async_computation.2 | async-start | bytes 4456448 | tf_op jit(solution)/shard_map/all_gather | solution.py:57
  359.8 317.2 %all-gather.15.cloned.1.call-start = ((), (), s32[]{:S(2)}) async-start(), calls=%async_computation.3 | async-start | bytes 18874368 | tf_op jit(solution)/shard_map/all_gather | solution.py:11
  571.0 5.7 copy-start.2
Sparse Core Ops, SparseCore 0:
  10.8 65.9 all-gather.16
  79.5 49.3 all-gather.8
  247.0 82.7 all-gather.10
  358.2 63.9 all-gather.18
  424.8 49.0 all-gather.12
  594.2 82.7 all-gather.14
